TPU v7x, 32 devices: a whole 2x2x4 slice. The times are simulated.
32 devices in a mesh: batch: 4 (over y, x), lat: 8 (over z, core).
Axes of the slice: x: 2, y: 2, z: 4, core: 2. Of those that a mesh axis runs over, the one named last changes fastest.
Arguments:
- patches: bfloat16 [8, 1024, 384], P('batch', 'lat'), may hold values from -6 to 6
- levels: int32 [8, 1024], P('batch', 'lat'), may hold values from 5 to 13, as said below
- lead_index: int32 [8], P('batch'), may hold values from 0 to 7
- lead_table: bfloat16 [8, 384], P('batch', 'lat'), may hold values from -5 to 5
- ada_weight: bfloat16 [2, 384, 2304], P(None, 'lat', 'batch'), may hold values from -0.3125 to 0.3125
- qkv_weight: bfloat16 [2, 384, 1152], P(None, 'lat', 'batch'), may hold values from -0.3125 to 0.3125
- out_weight: bfloat16 [2, 384, 384], P(None, 'lat', 'batch'), may hold values from -6 to 6
- up_weight: bfloat16 [2, 384, 1536], P(None, 'lat', 'batch'), may hold values from -0.3125 to 0.3125
- down_weight: bfloat16 [2, 1536, 384], P(None, 'lat', 'batch'), may hold values from -0.15625 to 0.15625
- cotangent: bfloat16 [8, 1024, 384], P('batch', 'lat'), may hold values from -6 to 6
Outputs:
- output: bfloat16 [8, 1024, 384], P('batch', 'lat')
- patches_grad: bfloat16 [8, 1024, 384], P('batch', 'lat')
- table_grad: float32 [8, 384], P('batch', 'lat')
- ada_grad: float32 [2, 384, 2304], P(None, 'lat', 'batch')
- qkv_grad: float32 [2, 384, 1152], P(None, 'lat', 'batch')
- out_grad: float32 [2, 384, 384], P(None, 'lat', 'batch')
- up_grad: float32 [2, 384, 1536], P(None, 'lat', 'batch')
- down_grad: float32 [2, 1536, 384], P(None, 'lat', 'batch')
Inputs may be any that keep to these rules, and one draw needn't show every extreme that they name: Patches among the first and last 128 positions of an item have at most 8 levels; every item has a patch with 5 and one with 13.
All inputs are finite; a program needn't handle non-finite values.
Results may differ from a plain program's by a relative error of at most 0.025.
Values may be sent and summed in bfloat16 or wider, within the bound.
No kernel may reach another device: no remote copies, remote signals or barrier semaphores. Data moves between devices by JAX's collectives and lax.ppermute only.
A program may use at most 192 MiB of HBM per device.

v0:
```python
import math

import jax
import jax.numpy as jnp
from jax import lax
from jax.sharding import PartitionSpec as P

HEADS = 6


eps = 1e-06
masked_score = -1e30
needed_levels = 9
highest = lax.Precision.HIGHEST


def layer_norm(stream):
    center = stream - jnp.mean(stream, axis=-1, keepdims=True)
    spread = jnp.mean(center * center, axis=-1, keepdims=True)
    return center * lax.rsqrt(spread + eps)


def norm_back(stream, upstream):
    return jax.vjp(layer_norm, stream)[1](upstream)[0]


def gelu_tanh(values):
    return jax.nn.gelu(values, approximate=True)


def gelu_back(values, upstream):
    return jax.vjp(gelu_tanh, values)[1](upstream)[0]


def low_dot(left, right):
    return jnp.dot(left, right, preferred_element_type=jnp.float32)


def dot_first(left, right):
    return lax.dot_general(
        left, right, (((0,), (0,)), ((), ())), preferred_element_type=jnp.float32
    )


def dot_second(left, right):
    return lax.dot_general(
        left, right, (((1,), (1,)), ((), ())), preferred_element_type=jnp.float32
    )


def to_heads(matrix, head_count):
    rows, width = matrix.shape
    return matrix.reshape(rows, head_count, width // head_count).transpose(1, 0, 2)


def from_heads(heads):
    head_count, rows, head_dim = heads.shape
    return heads.transpose(1, 0, 2).reshape(rows, head_count * head_dim)


def allowed(query_pos, key_pos, key_flags):
    return ((key_flags[None, :] > 0.5) | (query_pos[:, None] == key_pos[None, :]))[None]


def fold_block(
    state_now, key_heads, value_heads, key_flags, first_key, query_heads, query_pos, score_scale
):
    run_max, run_sum, weighted = state_now
    score = (
        jnp.einsum("hqd,hkd->hqk", query_heads, key_heads, preferred_element_type=jnp.float32)
        * score_scale
    )
    key_pos = first_key + jnp.arange(key_heads.shape[1], dtype=jnp.int32)
    permit = allowed(query_pos, key_pos, key_flags)
    score = jnp.where(permit, score, masked_score)
    new_max = jnp.maximum(run_max, jnp.max(score, axis=-1))
    exp_score = jnp.where(permit, jnp.exp(score - new_max[..., None]), 0.0)
    shrink = jnp.exp(run_max - new_max)
    run_sum = run_sum * shrink + jnp.sum(exp_score, axis=-1)
    weighted = weighted * shrink[..., None] + jnp.einsum(
        "hqk,hkd->hqd",
        exp_score.astype(jnp.bfloat16),
        value_heads,
        preferred_element_type=jnp.float32,
    )
    return (new_max, run_sum, weighted)


def attend_forward(query_heads, key_heads, value_heads, key_flags):
    head_count, query_rows, head_dim = query_heads.shape
    score_scale = 1.0 / math.sqrt(head_dim)
    query_pos = lax.axis_index("lat") * query_rows + jnp.arange(query_rows, dtype=jnp.int32)
    initial = (
        jnp.full((head_count, query_rows), masked_score, jnp.float32),
        jnp.zeros((head_count, query_rows), jnp.float32),
        jnp.zeros((head_count, query_rows, head_dim), jnp.float32),
    )
    flag_rows = key_flags[None, :]

    def visit(state_now, piece, first_key):
        key_piece, value_piece, flag_piece = piece
        total_rows = key_piece.shape[1]
        if total_rows > 1024 and total_rows % 1024 == 0:

            def scan_step(inner_state, block_index):
                start = block_index * 1024
                key_block = lax.dynamic_slice_in_dim(key_piece, start, 1024, 1)
                value_block = lax.dynamic_slice_in_dim(value_piece, start, 1024, 1)
                flag_block = lax.dynamic_slice_in_dim(flag_piece, start, 1024, 1)[0]
                return (
                    fold_block(
                        inner_state,
                        key_block,
                        value_block,
                        flag_block,
                        first_key + start,
                        query_heads,
                        query_pos,
                        score_scale,
                    ),
                    None,
                )

            state_now, unused = lax.scan(
                scan_step, state_now, jnp.arange(total_rows // 1024, dtype=jnp.int32)
            )
            return state_now
        return fold_block(
            state_now,
            key_piece,
            value_piece,
            flag_piece[0],
            first_key,
            query_heads,
            query_pos,
            score_scale,
        )

    run_max, run_sum, weighted = visit(
        initial,
        (
            lax.all_gather(key_heads, "lat", axis=1, tiled=True),
            lax.all_gather(value_heads, "lat", axis=1, tiled=True),
            lax.all_gather(flag_rows, "lat", axis=1, tiled=True),
        ),
        jnp.int32(0),
    )
    mix_heads = weighted / run_sum[..., None]
    log_total = run_max + jnp.log(run_sum)
    return (mix_heads, log_total)


def pair_grads(
    query_heads,
    grad_heads,
    log_total,
    row_delta,
    query_pos,
    key_heads,
    value_heads,
    key_flags,
    key_pos,
    score_scale,
):
    score = (
        jnp.einsum("hqd,hkd->hqk", query_heads, key_heads, preferred_element_type=jnp.float32)
        * score_scale
    )
    permit = allowed(query_pos, key_pos, key_flags)
    prob = jnp.where(permit, jnp.exp(score - log_total[..., None]), 0.0)
    prob_grad = jnp.einsum(
        "hqd,hkd->hqk", grad_heads, value_heads, preferred_element_type=jnp.float32
    )
    score_grad = (prob * (prob_grad - row_delta[..., None])).astype(jnp.bfloat16)
    value_part = jnp.einsum(
        "hqk,hqd->hkd", prob.astype(jnp.bfloat16), grad_heads, preferred_element_type=jnp.float32
    )
    key_part = (
        jnp.einsum("hqk,hqd->hkd", score_grad, query_heads, preferred_element_type=jnp.float32)
        * score_scale
    )
    query_part = (
        jnp.einsum("hqk,hkd->hqd", score_grad, key_heads, preferred_element_type=jnp.float32)
        * score_scale
    )
    return (query_part, key_part, value_part)


def attend_backward(
    query_heads, key_heads, value_heads, key_flags, mix_heads, log_total, grad_rows
):
    head_count, query_rows, head_dim = query_heads.shape
    score_scale = 1.0 / math.sqrt(head_dim)
    own_pos = lax.axis_index("lat") * query_rows + jnp.arange(query_rows, dtype=jnp.int32)
    grad_heads = to_heads(grad_rows, head_count)
    row_delta = jnp.sum(grad_heads.astype(jnp.float32) * mix_heads, axis=-1)
    key_all, value_all, flag_all = (
        lax.all_gather(key_heads, "lat", axis=1, tiled=True),
        lax.all_gather(value_heads, "lat", axis=1, tiled=True),
        lax.all_gather(key_flags, "lat", axis=0, tiled=True),
    )
    total_rows = key_all.shape[1]
    block_rows = 1024

    def key_step(carry, block_index):
        query_grad, key_acc, value_acc = carry
        start = block_index * block_rows
        key_block = lax.dynamic_slice_in_dim(key_all, start, block_rows, 1)
        value_block = lax.dynamic_slice_in_dim(value_all, start, block_rows, 1)
        flag_block = lax.dynamic_slice_in_dim(flag_all, start, block_rows, 0)
        key_pos = start + jnp.arange(block_rows, dtype=jnp.int32)
        query_part, key_part, value_part = pair_grads(
            query_heads,
            grad_heads,
            log_total,
            row_delta,
            own_pos,
            key_block,
            value_block,
            flag_block,
            key_pos,
            score_scale,
        )
        key_acc = lax.dynamic_update_slice_in_dim(key_acc, key_part, start, 1)
        value_acc = lax.dynamic_update_slice_in_dim(value_acc, value_part, start, 1)
        return ((query_grad + query_part, key_acc, value_acc), None)

    zero_all = jnp.zeros((head_count, total_rows, head_dim), jnp.float32)
    start_state = (jnp.zeros((head_count, query_rows, head_dim), jnp.float32), zero_all, zero_all)
    final_state, unused = lax.scan(
        key_step, start_state, jnp.arange(total_rows // block_rows, dtype=jnp.int32)
    )
    query_grad = final_state[0]
    key_grad, value_grad = (
        lax.psum_scatter(
            final_state[1].astype(jnp.bfloat16), "lat", scatter_dimension=1, tiled=True
        ).astype(jnp.float32),
        lax.psum_scatter(
            final_state[2].astype(jnp.bfloat16), "lat", scatter_dimension=1, tiled=True
        ).astype(jnp.float32),
    )
    joined = jnp.stack([query_grad, key_grad, value_grad])
    return (
        joined.transpose(2, 0, 1, 3)
        .reshape(query_rows, 3 * head_count * head_dim)
        .astype(jnp.bfloat16)
    )


def modulation_pieces(modulation, width):
    return [modulation[member * width : (member + 1) * width] for member in range(6)]


def layer_forward(stream, modulation, weights, key_flags, head_count):
    qkv_layer, out_layer, up_layer, down_layer = weights
    rows, width = stream.shape
    shift_one, scale_one, gate_one, shift_two, scale_two, gate_two = modulation_pieces(
        modulation, width
    )
    attn_in = (layer_norm(stream) * (1.0 + scale_one) + shift_one).astype(jnp.bfloat16)
    qkv = low_dot(attn_in, qkv_layer).astype(jnp.bfloat16)
    qkv_heads = qkv.reshape(rows, 3, head_count, width // head_count).transpose(1, 2, 0, 3)
    query_heads = qkv_heads[0]
    key_heads = qkv_heads[1]
    value_heads = qkv_heads[2]
    mix_heads, log_total = attend_forward(query_heads, key_heads, value_heads, key_flags)
    attn_low = from_heads(mix_heads).astype(jnp.bfloat16)
    branch_one = low_dot(attn_low, out_layer)
    middle = stream + gate_one * branch_one
    mlp_in = (layer_norm(middle) * (1.0 + scale_two) + shift_two).astype(jnp.bfloat16)
    up_proj = low_dot(mlp_in, up_layer)
    gelu_low = gelu_tanh(up_proj).astype(jnp.bfloat16)
    branch_two = low_dot(gelu_low, down_layer)
    result = middle + gate_two * branch_two
    kept = (
        stream,
        attn_in,
        query_heads,
        key_heads,
        value_heads,
        mix_heads,
        log_total,
        attn_low,
        branch_one,
        middle,
        mlp_in,
        up_proj,
        gelu_low,
        branch_two,
    )
    return (result, kept)


def layer_backward(upstream, modulation, weights, kept, key_flags):
    qkv_layer, out_layer, up_layer, down_layer = weights
    (
        stream,
        attn_in,
        query_heads,
        key_heads,
        value_heads,
        mix_heads,
        log_total,
        attn_low,
        branch_one,
        middle,
        mlp_in,
        up_proj,
        gelu_low,
        branch_two,
    ) = kept
    width = stream.shape[1]
    shift_one, scale_one, gate_one, shift_two, scale_two, gate_two = modulation_pieces(
        modulation, width
    )
    gate_two_grad = jnp.sum(upstream * branch_two, axis=0)
    branch_two_grad = (gate_two * upstream).astype(jnp.bfloat16)
    down_part = dot_first(gelu_low, branch_two_grad)
    gelu_grad = dot_second(branch_two_grad, down_layer)
    up_grad_low = gelu_back(up_proj, gelu_grad).astype(jnp.bfloat16)
    up_part = dot_first(mlp_in, up_grad_low)
    mlp_grad = dot_second(up_grad_low, up_layer)
    shift_two_grad = jnp.sum(mlp_grad, axis=0)
    scale_two_grad = jnp.sum(mlp_grad * layer_norm(middle), axis=0)
    middle_grad = upstream + norm_back(middle, mlp_grad * (1.0 + scale_two))
    gate_one_grad = jnp.sum(middle_grad * branch_one, axis=0)
    branch_one_grad = (gate_one * middle_grad).astype(jnp.bfloat16)
    out_part = dot_first(attn_low, branch_one_grad)
    attn_grad = dot_second(branch_one_grad, out_layer).astype(jnp.bfloat16)
    qkv_grad_low = attend_backward(
        query_heads, key_heads, value_heads, key_flags, mix_heads, log_total, attn_grad
    )
    qkv_part = dot_first(attn_in, qkv_grad_low)
    in_grad = dot_second(qkv_grad_low, qkv_layer)
    shift_one_grad = jnp.sum(in_grad, axis=0)
    scale_one_grad = jnp.sum(in_grad * layer_norm(stream), axis=0)
    stream_grad = middle_grad + norm_back(stream, in_grad * (1.0 + scale_one))
    modulation_grad = jnp.concatenate(
        [
            shift_one_grad,
            scale_one_grad,
            gate_one_grad,
            shift_two_grad,
            scale_two_grad,
            gate_two_grad,
        ]
    )
    return (stream_grad, (qkv_part, out_part, up_part, down_part), modulation_grad)


def run_micro(patch_rows, level_row, lead_value, cotan_rows, whole):
    table_full, ada_full, qkv_full, out_full, up_full, down_full = whole
    width = patch_rows.shape[1]
    layer_count = qkv_full.shape[0]
    lead_hot = (lead_value == jnp.arange(table_full.shape[0], dtype=jnp.int32)).astype(jnp.float32)
    embed = jnp.dot(lead_hot[None, :], table_full.astype(jnp.float32), precision=highest)[0]
    cond_low = jax.nn.silu(embed).astype(jnp.bfloat16)
    key_flags = (level_row >= needed_levels).astype(jnp.bfloat16)
    stream = patch_rows.astype(jnp.float32)
    saved = []
    for layer_number in range(layer_count):
        modulation = low_dot(cond_low[None, :], ada_full[layer_number])[0]
        weights = (
            qkv_full[layer_number],
            out_full[layer_number],
            up_full[layer_number],
            down_full[layer_number],
        )
        stream, kept = layer_forward(stream, modulation, weights, key_flags, HEADS)
        saved.append((modulation, kept))
    result = stream.astype(jnp.bfloat16)
    upstream = cotan_rows.astype(jnp.float32)
    cond_grad = jnp.zeros((width,), jnp.float32)
    ada_parts = [None] * layer_count
    qkv_parts = [None] * layer_count
    out_parts = [None] * layer_count
    up_parts = [None] * layer_count
    down_parts = [None] * layer_count
    for layer_number in reversed(range(layer_count)):
        modulation, kept = saved[layer_number]
        weights = (
            qkv_full[layer_number],
            out_full[layer_number],
            up_full[layer_number],
            down_full[layer_number],
        )
        upstream, parts, modulation_grad = layer_backward(
            upstream, modulation, weights, kept, key_flags
        )
        (
            qkv_parts[layer_number],
            out_parts[layer_number],
            up_parts[layer_number],
            down_parts[layer_number],
        ) = parts
        ada_parts[layer_number] = cond_low.astype(jnp.float32)[:, None] * modulation_grad[None, :]
        cond_grad = cond_grad + jnp.dot(
            ada_full[layer_number].astype(jnp.float32), modulation_grad, precision=highest
        )
    embed_grad = jax.vjp(jax.nn.silu, embed)[1](cond_grad)[0]
    table_part = lead_hot[:, None] * embed_grad[None, :]
    grads = (
        table_part,
        jnp.stack(ada_parts),
        jnp.stack(qkv_parts),
        jnp.stack(out_parts),
        jnp.stack(up_parts),
        jnp.stack(down_parts),
    )
    return (result, upstream.astype(jnp.bfloat16), grads)


def collect(lead_table, ada_weight, qkv_weight, out_weight, up_weight, down_weight):
    by_lat = (
        lax.all_gather(lead_table, "lat", axis=1, tiled=True),
        lax.all_gather(ada_weight, "lat", axis=1, tiled=True),
        lax.all_gather(qkv_weight, "lat", axis=1, tiled=True),
        lax.all_gather(out_weight, "lat", axis=1, tiled=True),
        lax.all_gather(up_weight, "lat", axis=1, tiled=True),
        lax.all_gather(down_weight, "lat", axis=1, tiled=True),
    )
    return (
        lax.all_gather(by_lat[0], "batch", axis=0, tiled=True),
        lax.all_gather(by_lat[1], "batch", axis=2, tiled=True),
        lax.all_gather(by_lat[2], "batch", axis=2, tiled=True),
        lax.all_gather(by_lat[3], "batch", axis=2, tiled=True),
        lax.all_gather(by_lat[4], "batch", axis=2, tiled=True),
        lax.all_gather(by_lat[5], "batch", axis=2, tiled=True),
    )


def spread_grads(grads):
    by_batch = (
        lax.psum_scatter(
            grads[0].astype(jnp.bfloat16), "batch", scatter_dimension=0, tiled=True
        ).astype(jnp.float32),
        lax.psum_scatter(
            grads[1].astype(jnp.bfloat16), "batch", scatter_dimension=2, tiled=True
        ).astype(jnp.float32),
        lax.psum_scatter(
            grads[2].astype(jnp.bfloat16), "batch", scatter_dimension=2, tiled=True
        ).astype(jnp.float32),
        lax.psum_scatter(
            grads[3].astype(jnp.bfloat16), "batch", scatter_dimension=2, tiled=True
        ).astype(jnp.float32),
        lax.psum_scatter(
            grads[4].astype(jnp.bfloat16), "batch", scatter_dimension=2, tiled=True
        ).astype(jnp.float32),
        lax.psum_scatter(
            grads[5].astype(jnp.bfloat16), "batch", scatter_dimension=2, tiled=True
        ).astype(jnp.float32),
    )
    return (
        lax.psum_scatter(
            by_batch[0].astype(jnp.bfloat16), "lat", scatter_dimension=1, tiled=True
        ).astype(jnp.float32),
        lax.psum_scatter(
            by_batch[1].astype(jnp.bfloat16), "lat", scatter_dimension=1, tiled=True
        ).astype(jnp.float32),
        lax.psum_scatter(
            by_batch[2].astype(jnp.bfloat16), "lat", scatter_dimension=1, tiled=True
        ).astype(jnp.float32),
        lax.psum_scatter(
            by_batch[3].astype(jnp.bfloat16), "lat", scatter_dimension=1, tiled=True
        ).astype(jnp.float32),
        lax.psum_scatter(
            by_batch[4].astype(jnp.bfloat16), "lat", scatter_dimension=1, tiled=True
        ).astype(jnp.float32),
        lax.psum_scatter(
            by_batch[5].astype(jnp.bfloat16), "lat", scatter_dimension=1, tiled=True
        ).astype(jnp.float32),
    )


def add_tuples(first_terms, second_terms):
    return tuple(
        (first_term + second_term for first_term, second_term in zip(first_terms, second_terms))
    )


def per_device(
    patches,
    levels,
    lead_index,
    lead_table,
    ada_weight,
    qkv_weight,
    out_weight,
    up_weight,
    down_weight,
    cotangent,
):
    micro_count = patches.shape[0]
    results = []
    input_grads = []
    shards = None
    for micro_index in range(micro_count):
        whole = collect(lead_table, ada_weight, qkv_weight, out_weight, up_weight, down_weight)
        result, back_rows, grads = run_micro(
            patches[micro_index],
            levels[micro_index],
            lead_index[micro_index],
            cotangent[micro_index],
            whole,
        )
        results.append(result)
        input_grads.append(back_rows)
        portion = spread_grads(grads)
        shards = portion if shards is None else add_tuples(shards, portion)
    return (
        jnp.stack(results),
        jnp.stack(input_grads),
        shards[0],
        shards[1],
        shards[2],
        shards[3],
        shards[4],
        shards[5],
    )


def solution(mesh):
    return jax.shard_map(
        per_device,
        mesh=mesh,
        in_specs=(
            P("batch", "lat", None),
            P("batch", "lat"),
            P("batch"),
            P("batch", "lat"),
            P(None, "lat", "batch"),
            P(None, "lat", "batch"),
            P(None, "lat", "batch"),
            P(None, "lat", "batch"),
            P(None, "lat", "batch"),
            P("batch", "lat", None),
        ),
        out_specs=(
            P("batch", "lat", None),
            P("batch", "lat", None),
            P("batch", "lat"),
            P(None, "lat", "batch"),
            P(None, "lat", "batch"),
            P(None, "lat", "batch"),
            P(None, "lat", "batch"),
            P(None, "lat", "batch"),
        ),
        check_vma=False,
    )
```

profile of v0, /device:TPU:0, one launch (start us, length us, event | category | flops | bytes accessed | tf_op | source)
XLA Modules:
  0.0 1454.1 jit_solution(15833717541636194697)
XLA Ops:
  8.2 16.6 %all_gather.101 = bf16[2,384,288]{2,0,1:T(2,128)(2,1)S(1)} all-gather(bf16[2,48,288]{2,0,1:T(2,128)(2,1)S(1)} %copy.91), channel_id=1, replica_groups=mesh['batch'=4,'lat'=8] {'lat'}, dimensions={1}, use_global_device_ids=true | all-gather | bytes 497664 | tf_op jit(solution)/shard_map/all_gather | solution.py:417
  27.7 15.7 %all_gather.109 = bf16[2,1536,96]{2,0,1:T(2,128)(2,1)S(1)} all-gather(bf16[2,192,96]{2,0,1:T(2,128)(2,1)S(1)} %copy.98), channel_id=1, replica_groups=mesh['batch'=4,'lat'=8] {'lat'}, dimensions={1}, use_global_device_ids=true | all-gather | bytes 663552 | tf_op jit(solution)/shard_map/all_gather | solution.py:420
  45.5 17.5 %all_gather.98 = bf16[2,384,576]{2,0,1:T(2,128)(2,1)S(1)} all-gather(bf16[2,48,576]{2,0,1:T(2,128)(2,1)S(1)} %copy.88), channel_id=1, replica_groups=mesh['batch'=4,'lat'=8] {'lat'}, dimensions={1}, use_global_device_ids=true | all-gather | bytes 995328 | tf_op jit(solution)/shard_map/all_gather | solution.py:416
  66.1 16.4 %all_gather.107 = bf16[2,384,384]{2,1,0:T(8,128)(2,1)} all-gather(bf16[2,48,384]{2,1,0:T(8,128)(2,1)S(1)} %copy-done.124), channel_id=1, replica_groups=mesh['batch'=4,'lat'=8] {'lat'}, dimensions={1}, use_global_device_ids=true | all-gather | bytes 663552 | tf_op jit(solution)/shard_map/all_gather | solution.py:419
  82.6 11.9 all-gather.8
  94.5 8.7 all_gather.100
  103.2 10.0 all-gather.9
  113.3 8.7 all_gather.113
  123.8 10.1 all-gather.10
  134.0 8.4 all-gather.11
  145.2 14.1 all_gather.105
  159.5 13.3 all_gather.106
  191.9 9.0 fusion.373
  200.9 6.5 copy.164
  207.4 6.5 copy.160
  213.9 8.7 fusion.372
  222.6 7.3 copy.157
  232.2 14.9 %all-gather = bf16[1,6,1024,64]{2,3,1,0:T(8,128)(2,1)S(1)} all-gather(bf16[1,6,128,64]{2,3,1,0:T(8,128)(2,1)S(1)} %get-tuple-element.275), channel_id=2, replica_groups=mesh['batch'=4,'lat'=8] {'lat'}, dimensions={2}, use_global_device_ids=true | all-gather | bytes 884736 | tf_op jit(solution)/shard_map/all_gather | solution.py:142
  250.2 7.3 copy.161
  264.3 15.5 %all-gather.4 = bf16[1,6,1024,64]{2,3,1,0:T(8,128)(2,1)S(1)} all-gather(bf16[1,6,128,64]{2,3,1,0:T(8,128)(2,1)S(1)} %get-tuple-element.279), channel_id=6, replica_groups=mesh['batch'=4,'lat'=8] {'lat'}, dimensions={2}, use_global_device_ids=true | all-gather | bytes 884736 | tf_op jit(solution)/shard_map/all_gather | solution.py:142
  284.1 15.4 %all-gather.5 = bf16[1,6,1024,64]{2,3,1,0:T(8,128)(2,1)S(1)} all-gather(bf16[1,6,128,64]{2,3,1,0:T(8,128)(2,1)S(1)} %get-tuple-element.278), channel_id=7, replica_groups=mesh['batch'=4,'lat'=8] {'lat'}, dimensions={2}, use_global_device_ids=true | all-gather | bytes 884736 | tf_op jit(solution)/shard_map/all_gather | solution.py:143
  301.6 15.4 %all-gather.1 = bf16[1,6,1024,64]{2,3,1,0:T(8,128)(2,1)S(1)} all-gather(bf16[1,6,128,64]{2,3,1,0:T(8,128)(2,1)S(1)} %copy-done.113), channel_id=3, replica_groups=mesh['batch'=4,'lat'=8] {'lat'}, dimensions={2}, use_global_device_ids=true | all-gather | bytes 884736 | tf_op jit(solution)/shard_map/all_gather | solution.py:143
  335.0 16.0 %all-gather.2 = bf16[1,6,1024,64]{2,3,1,0:T(8,128)(2,1)S(1)} all-gather(bf16[1,6,128,64]{2,3,1,0:T(8,128)(2,1)S(1)} %get-tuple-element.273), channel_id=4, replica_groups=mesh['batch'=4,'lat'=8] {'lat'}, dimensions={2}, use_global_device_ids=true | all-gather | bytes 884736 | tf_op jit(solution)/shard_map/all_gather | solution.py:142
  363.6 15.6 %all-gather.6 = bf16[1,6,1024,64]{2,3,1,0:T(8,128)(2,1)S(1)} all-gather(bf16[1,6,128,64]{2,3,1,0:T(8,128)(2,1)S(1)} %get-tuple-element.277), channel_id=8, replica_groups=mesh['batch'=4,'lat'=8] {'lat'}, dimensions={2}, use_global_device_ids=true | all-gather | bytes 884736 | tf_op jit(solution)/shard_map/all_gather | solution.py:142
  383.5 15.4 %all-gather.3 = bf16[1,6,1024,64]{2,3,1,0:T(8,128)(2,1)S(1)} all-gather(bf16[1,6,128,64]{2,3,1,0:T(8,128)(2,1)S(1)} %copy-done.114), channel_id=5, replica_groups=mesh['batch'=4,'lat'=8] {'lat'}, dimensions={2}, use_global_device_ids=true | all-gather | bytes 884736 | tf_op jit(solution)/shard_map/all_gather | solution.py:143
  398.9 16.4 %all-gather.7 = bf16[1,6,1024,64]{2,3,1,0:T(8,128)(2,1)} all-gather(bf16[1,6,128,64]{2,3,1,0:T(8,128)(2,1)S(1)} %get-tuple-element.276), channel_id=9, replica_groups=mesh['batch'=4,'lat'=8] {'lat'}, dimensions={2}, use_global_device_ids=true | all-gather | bytes 884736 | tf_op jit(solution)/shard_map/all_gather | solution.py:143
  507.3 29.0 %reduce-scatter.69.cloned.1.call-done = bf16[128,384]{1,0:T(8,128)(2,1)} async-done(((bf16[1024,384]{1,0:T(8,128)(2,1)}), bf16[128,384]{1,0:T(8,128)(2,1)}) %reduce-scatter.69.cloned.1.call-update) | async-done | bytes 98320
  547.0 21.9 %reduce-scatter.71.cloned.1.call-done = bf16[128,384]{1,0:T(8,128)(2,1)} async-done(((bf16[1024,384]{1,0:T(8,128)(2,1)}), bf16[128,384]{1,0:T(8,128)(2,1)}) %reduce-scatter.71.cloned.1.call-update) | async-done | bytes 98320
  655.1 6.9 copy.151
  670.8 6.9 copy.149
  711.0 22.7 %reduce-scatter.75.cloned.1.call-done = bf16[128,384]{1,0:T(8,128)(2,1)} async-done(((bf16[1024,384]{1,0:T(8,128)(2,1)}), bf16[128,384]{1,0:T(8,128)(2,1)}) %reduce-scatter.75.cloned.1.call-update) | async-done | bytes 98320
  749.1 10.5 copy.147
  775.7 10.7 copy.145
  813.1 6.9 copy.121
  823.5 6.9 copy.120
  836.6 6.6 copy.112
  847.3 6.6 copy.114
  866.2 16.4 %all-reduce.13 = (bf16[8,384]{1,0:T(8,128)(2,1)S(1)}, bf16[8,384]{1,0:T(8,128)(2,1)S(1)}) all-reduce(bf16[8,384]{1,0:T(8,128)(2,1)S(1)} %multiply_convert_fusion.34, bf16[8,384]{1,0:T(8,128)(2,1)S(1)} %multiply_convert_fusion.35), channel_id=22, replica_groups=mesh['batch'=4,'lat'=8] {'batch'}, use_global_device_ids=true, to_apply=%region_78.79.clone | all-reduce | flops 6144 | bytes 24576
  896.9 16.3 %reduce-scatter.81.cloned.1.call-done = bf16[576,768]{1,0:T(8,128)(2,1)} async-done(((bf16[2304,768]{1,0:T(8,128)(2,1)}), bf16[576,768]{1,0:T(8,128)(2,1)}) %reduce-scatter.81.cloned.1.call-update) | async-done | bytes 884752
  919.0 187.1 %all-reduce.20.cloned.1.call-done = (bf16[2,384,1152]{1,0,2:T(2,128)(2,1)}, bf16[2,384,1152]{1,0,2:T(2,128)(2,1)}, bf16[2,384,384]{1,0,2:T(2,128)(2,1)}, bf16[2,...) async-done(((bf16[2,384,1152]{1,0,2:T(2,128)(2,1)}, bf16[2,384,1152]{1,0,2:T(2,128)(2,1)}, bf16[2,384,384]{1,0,2:T(2,128)(2,1)}, ...) | async-done | bytes 9437200
  1118.0 58.2 %copy.153 = bf16[2,1536,96]{0,2,1:T(8,128)(2,1)} copy(bf16[2,1536,96]{1,0,2:T(2,128)(2,1)S(1)} %constant_dynamic-slice_fusion.1) | data formatting | bytes 1179648
  1176.2 56.6 %reshape.935 = bf16[1536,192]{1,0:T(8,128)(2,1)} reshape(bf16[1536,96,2]{2,1,0:T(8,128)(2,1)} %bitcast.605) | data formatting | bytes 1179648
  1236.5 58.2 %copy.155 = bf16[2,1536,96]{0,2,1:T(8,128)(2,1)} copy(bf16[2,1536,96]{1,0,2:T(2,128)(2,1)S(1)} %constant_dynamic-slice_fusion.4) | data formatting | bytes 1179648
  1294.8 56.6 %reshape.937 = bf16[1536,192]{1,0:T(8,128)(2,1)} reshape(bf16[1536,96,2]{2,1,0:T(8,128)(2,1)} %bitcast.606) | data formatting | bytes 1179648
  1366.4 30.3 %reduce-scatter.89.cloned.1.call-done = bf16[192,192]{1,0:T(8,128)(2,1)} async-done(((bf16[1536,192]{1,0:T(8,128)(2,1)}), bf16[192,192]{1,0:T(8,128)(2,1)}) %reduce-scatter.89.cloned.1.call-update) | async-done | bytes 73744
  1396.8 11.6 reshape.936
  1414.0 15.2 %reduce-scatter.91.cloned.1.call-done = bf16[192,192]{1,0:T(8,128)(2,1)} async-done(((bf16[1536,192]{1,0:T(8,128)(2,1)}), bf16[192,192]{1,0:T(8,128)(2,1)}) %reduce-scatter.91.cloned.1.call-update) | async-done | bytes 73744
  1429.2 11.6 reshape.938
  (858 shorter events, 459.2 us)
Async XLA Ops:
  7.2 171.1 %all-gather.19.cloned.1.call-start = ((), (), s32[]{:S(2)}) async-start(), calls=%async_computation.21 | async-start | bytes 2211840 | tf_op jit(solution)/shard_map/all_gather | solution.py:425
  26.6 165.3 %all-gather.23.cloned.1.call-start = ((), (), s32[]{:S(2)}) async-start(), calls=%async_computation.23 | async-start | bytes 2949120 | tf_op jit(solution)/shard_map/all_gather | solution.py:428
  45.3 168.5 %all-gather.17.cloned.1.call-start = ((), (), s32[]{:S(2)}) async-start(), calls=%async_computation.20 | async-start | bytes 4423680 | tf_op jit(solution)/shard_map/all_gather | solution.py:424
  45.5 76.5 %copy-start.212 = (s32[2]{0:T(128)S(1)}, s32[2]{0:T(128)}, u32[]{:S(2)}) copy-start(s32[2]{0:T(128)} %param.12) | copy-start | bytes 28
  45.5 77.2 %copy-start.11 = (bf16[2,128,384]{2,1,0:T(8,128)(2,1)S(1)}, bf16[2,128,384]{2,1,0:T(8,128)(2,1)}, u32[]{:S(2)}) copy-start(bf16[2,128,384]{2,1,0:T(8,128)(2,1)} %param.10) | copy-start | bytes 589828
  63.1 60.7 %copy-start.227 = (bf16[2,48]{1,0:T(2,128)(2,1)S(1)}, bf16[2,48]{1,0:T(2,128)(2,1)}, u32[]{:S(2)}) copy-start(bf16[2,48]{1,0:T(2,128)(2,1)} %param.13) | copy-start | bytes 580
  63.1 82.0 %copy-start.141 = (bf16[2,48,96]{2,1,0:T(8,128)(2,1)S(1)}, bf16[2,48,96]{2,1,0:T(8,128)(2,1)}, u32[]{:S(2)}) copy-start(bf16[2,48,96]{2,1,0:T(8,128)(2,1)} %param.16) | copy-start | bytes 55300
  66.1 257.8 %all-gather.21.cloned.1.call-start = ((), (), s32[]{:S(2)}) async-start(), calls=%async_computation.22 | async-start | bytes 2949120 | tf_op jit(solution)/shard_map/all_gather | solution.py:427
  82.6 415.5 %reduce-scatter.61.cloned.1.call-start = ((), (), s32[]{:S(2)}) async-start(), calls=%async_computation.28 | async-start | bytes 884736
  122.8 108.1 %copy-start.142 = (f32[128]{0:T(128)}, f32[128]{0:T(128)S(1)}, u32[]{:S(2)}) copy-start(f32[128]{0:T(128)S(1)} %broadcast_multiply_fusion.7) | copy-start | bytes 1540
  123.1 107.9 %copy-start.173 = (f32[128]{0:T(128)}, f32[128]{0:T(128)S(1)}, u32[]{:S(2)}) copy-start(f32[128]{0:T(128)S(1)} %fusion.310) | copy-start | bytes 1540
  144.5 85.4 %copy-start.165 = (bf16[384,1]{0,1:T(2,128)(2,1)}, bf16[384,1]{0,1:T(2,128)(2,1)S(1)}, u32[]{:S(2)}) copy-start(bf16[384,1]{0,1:T(2,128)(2,1)S(1)} %reshape.889) | copy-start | bytes 2308
  145.1 112.5 %copy-start.167 = (bf16[384,1]{0,1:T(2,128)(2,1)}, bf16[384,1]{0,1:T(2,128)(2,1)S(1)}, u32[]{:S(2)}) copy-start(bf16[384,1]{0,1:T(2,128)(2,1)S(1)} %reshape.895) | copy-start | bytes 2308
  178.2 69.8 %copy-start.50 = (pred[128,1024]{1,0:T(8,128)(4,1)}, pred[128,1024]{1,0:T(8,128)(4,1)S(1)}, u32[]{:S(2)}) copy-start(pred[128,1024]{1,0:T(8,128)(4,1)S(1)} %get-tuple-element.343) | copy-start | bytes 393220
  230.9 88.0 %copy-start.129 = (f32[384]{0:T(512)}, f32[384]{0:T(512)S(1)}, u32[]{:S(2)}) copy-start(f32[384]{0:T(512)S(1)} %get-tuple-element.297) | copy-start | bytes 4612
  258.6 60.3 %copy-start.132 = (f32[384]{0:T(512)}, f32[384]{0:T(512)S(1)}, u32[]{:S(2)}) copy-start(f32[384]{0:T(512)S(1)} %get-tuple-element.309) | copy-start | bytes 4612
  441.9 61.9 %reduce-scatter.63.cloned.1.call-start = ((), (), s32[]{:S(2)}) async-start(), calls=%async_computation.29 | async-start | bytes 884736
  458.1 78.3 %reduce-scatter.69.cloned.1.call-start = ((), (), s32[]{:S(2)}) async-start(), calls=%async_computation.32 | async-start | bytes 884736
  482.5 86.4 %reduce-scatter.71.cloned.1.call-start = ((), (), s32[]{:S(2)}) async-start(), calls=%async_computation.33 | async-start | bytes 884736
  493.6 206.8 %reduce-scatter.65.cloned.1.call-start = ((), (), s32[]{:S(2)}) async-start(), calls=%async_computation.30 | async-start | bytes 884736
  606.0 97.9 %reduce-scatter.67.cloned.1.call-start = ((), (), s32[]{:S(2)}) async-start(), calls=%async_computation.31 | async-start | bytes 884736
  617.0 90.4 %reduce-scatter.73.cloned.1.call-start = ((), (), s32[]{:S(2)}) async-start(), calls=%async_computation.34 | async-start | bytes 884736
  639.0 94.7 %reduce-scatter.75.cloned.1.call-start = ((), (), s32[]{:S(2)}) async-start(), calls=%async_computation.35 | async-start | bytes 884736
  650.0 234.3 %reduce-scatter.87.cloned.1.call-start = ((), (), s32[]{:S(2)}) async-start(), calls=%async_computation.41 | async-start | bytes 2949120
  665.7 222.7 %reduce-scatter.85.cloned.1.call-start = ((), (), s32[]{:S(2)}) async-start(), calls=%async_computation.40 | async-start | bytes 2949120
  683.9 208.4 %reduce-scatter.83.cloned.1.call-start = ((), (), s32[]{:S(2)}) async-start(), calls=%async_computation.39 | async-start | bytes 4423680
  764.0 149.2 %reduce-scatter.81.cloned.1.call-start = ((), (), s32[]{:S(2)}) async-start(), calls=%async_computation.38 | async-start | bytes 4423680
  790.9 315.3 %all-reduce.20.cloned.1.call-start = ((), (), s32[]{:S(2)}) async-start(), calls=%async_computation.45 | async-start | bytes 18874368
  853.9 498.5 %reduce-scatter.77.cloned.1.call-start = ((), (), s32[]{:S(2)}) async-start(), calls=%async_computation.36 | async-start | bytes 110592
  883.4 469.8 %reduce-scatter.79.cloned.1.call-start = ((), (), s32[]{:S(2)}) async-start(), calls=%async_computation.37 | async-start | bytes 110592
  884.3 470.3 %reduce-scatter.59.cloned.1.call-start = ((), (), s32[]{:S(2)}) async-start(), calls=%async_computation.27 | async-start | bytes 663552 | tf_op jit(solution)/shard_map/reduce_scatter | solution.py:466
  888.1 466.4 %reduce-scatter.57.cloned.1.call-start = ((), (), s32[]{:S(2)}) async-start(), calls=%async_computation.26 | async-start | bytes 663552 | tf_op jit(solution)/shard_map/reduce_scatter | solution.py:466
  892.2 464.0 %reduce-scatter.55.cloned.1.call-start = ((), (), s32[]{:S(2)}) async-start(), calls=%async_computation.25 | async-start | bytes 1105920 | tf_op jit(solution)/shard_map/reduce_scatter | solution.py:457
  896.8 459.4 %reduce-scatter.53.cloned.1.call-start = ((), (), s32[]{:S(2)}) async-start(), calls=%async_computation.24 | async-start | bytes 1105920 | tf_op jit(solution)/shard_map/reduce_scatter | solution.py:457
  917.7 445.7 %all-reduce.18.cloned.1.call-start = ((), (), s32[]{:S(2)}) async-start(), calls=%async_computation.44 | async-start | bytes 3145728
  1116.5 280.3 %reduce-scatter.89.cloned.1.call-start = ((), (), s32[]{:S(2)}) async-start(), calls=%async_computation.42 | async-start | bytes 884736
  1176.2 56.9 %copy-start.228 = (u32[32]{0:T(128)S(1)}, u32[32]{0:T(128)}, u32[]{:S(2)}) copy-start(u32[32]{0:T(128)} %constant.172) | copy-start | bytes 388
  1176.2 58.1 %copy-start.111 = (bf16[1,128,384]{2,1,0:T(8,128)(2,1)S(1)}, bf16[1,128,384]{2,1,0:T(8,128)(2,1)}, u32[]{:S(2)}) copy-start(bf16[1,128,384]{2,1,0:T(8,128)(2,1)} %get-tuple-element.282) | copy-start | bytes 294916
  1176.2 58.1 %copy-start.112 = (bf16[1,128,384]{2,1,0:T(8,128)(2,1)S(1)}, bf16[1,128,384]{2,1,0:T(8,128)(2,1)}, u32[]{:S(2)}) copy-start(bf16[1,128,384]{2,1,0:T(8,128)(2,1)} %get-tuple-element.283) | copy-start | bytes 294916
  1176.2 58.8 %copy-start.217 = (f32[128]{0:T(128)S(1)}, f32[128]{0:T(128)}, u32[]{:S(2)}) copy-start(f32[128]{0:T(128)} %get-tuple-element.153) | copy-start | bytes 1540
  1176.2 58.8 %copy-start.216 = (f32[128]{0:T(128)S(1)}, f32[128]{0:T(128)}, u32[]{:S(2)}) copy-start(f32[128]{0:T(128)} %get-tuple-element.193) | copy-start | bytes 1540
  1232.8 196.4 %reduce-scatter.91.cloned.1.call-start = ((), (), s32[]{:S(2)}) async-start(), calls=%async_computation.43 | async-start | bytes 884736
  1294.7 56.7 %copy-start.76 = (f32[128,384]{1,0:T(8,128)S(1)}, f32[128,384]{1,0:T(8,128)}, u32[]{:S(2)}) copy-start(f32[128,384]{1,0:T(8,128)} %copy-done.75) | copy-start | bytes 589828
  1294.7 56.7 %copy-start.144 = (f32[128]{0:T(128)S(1)}, f32[128]{0:T(128)}, u32[]{:S(2)}) copy-start(f32[128]{0:T(128)} %copy-done.142) | copy-start | bytes 1540
  1294.8 56.7 %copy-start.175 = (f32[128]{0:T(128)S(1)}, f32[128]{0:T(128)}, u32[]{:S(2)}) copy-start(f32[128]{0:T(128)} %copy-done.173) | copy-start | bytes 1540
  1294.8 56.7 %copy-start.176 = (f32[128]{0:T(128)S(1)}, f32[128]{0:T(128)}, u32[]{:S(2)}) copy-start(f32[128]{0:T(128)} %fusion.314) | copy-start | bytes 1540
  1294.8 56.7 %copy-start.204 = (f32[128]{0:T(128)S(1)}, f32[128]{0:T(128)}, u32[]{:S(2)}) copy-start(f32[128]{0:T(128)} %copy-done.203) | copy-start | bytes 1540
  1294.8 56.7 %copy-start.206 = (f32[128]{0:T(128)S(1)}, f32[128]{0:T(128)}, u32[]{:S(2)}) copy-start(f32[128]{0:T(128)} %copy-done.205) | copy-start | bytes 1540
  (208 other events, 1449.7 us)
Sparse Core Ops, SparseCore 0:
  26.7 33.5 all-gather.18
  62.2 37.3 all-gather.22
  101.4 47.1 all-gather.16
  150.3 41.6 all-gather.20
  442.0 29.4 reduce-scatter.60
  473.6 30.1 reduce-scatter.62
  506.1 30.2 reduce-scatter.68
  538.6 30.2 reduce-scatter.70
  606.1 30.1 reduce-scatter.64
  638.4 30.2 reduce-scatter.66
  671.0 30.2 reduce-scatter.72
  703.5 30.1 reduce-scatter.74
  736.8 35.6 reduce-scatter.86
  775.4 37.3 reduce-scatter.84
  815.7 47.1 reduce-scatter.82
  865.8 47.3 reduce-scatter.80
  917.5 188.5 all-reduce.19
  1108.8 30.5 reduce-scatter.76
  1142.2 28.7 reduce-scatter.78
  1173.1 29.6 reduce-scatter.58
  1205.1 29.6 reduce-scatter.56
  1237.0 30.4 reduce-scatter.54
  1269.8 30.5 reduce-scatter.52
  1302.9 60.3 all-reduce.17
  1365.6 31.1 reduce-scatter.88
  1398.9 30.2 reduce-scatter.90
where the time goes:
time: 1470 us; the launch traced here: 1450 us
  local copies, waits for them, and re-layouts  604 us (41%)
  waiting for transfers between devices  331 us (23%)
  blocking collectives  292 us (20%)
  matrix products  135 us (9%)
  other arithmetic  69.3 us (5%)
  between operations  19.9 us (1%)
    unnamed x567, local copies, waits for them, and re-layouts  512 us
    unnamed x44, waiting for transfers between devices  331 us
    all_gather x4, blocking collectives, attend_forward(): lax.all_gather(value_heads, 'lat', axis=1, tiled=True)  62.7 us
    all_gather x4, blocking collectives, attend_forward(): lax.all_gather(key_heads, 'lat', axis=1, tiled=True)  61.9 us
  transfers between devices with their start and end apart: 26, of which 9 were waited for; matrix products, arithmetic and copies ran while one was open for 47% of the time, Pallas kernels for 0%

commit v1 on v0

v1 whole, which is shorter than its diff:
```python
import math

import jax
import jax.numpy as jnp
from jax import lax
from jax.sharding import PartitionSpec as P

HEADS = 6
eps = 1e-06
masked_score = -1e30
needed_levels = 9
highest = lax.Precision.HIGHEST
bf16 = jnp.bfloat16
f32 = jnp.float32


def layer_norm(stream):
    center = stream - jnp.mean(stream, axis=-1, keepdims=True)
    spread = jnp.mean(center * center, axis=-1, keepdims=True)
    return center * lax.rsqrt(spread + eps)


def norm_back(stream, upstream):
    return jax.vjp(layer_norm, stream)[1](upstream)[0]


def gelu_tanh(values):
    return jax.nn.gelu(values, approximate=True)


def gelu_back(values, upstream):
    return jax.vjp(gelu_tanh, values)[1](upstream)[0]


def low_dot(left, right):
    return jnp.dot(left, right, preferred_element_type=f32)


def dot_first(left, right):
    return lax.dot_general(left, right, (((0,), (0,)), ((), ())), preferred_element_type=f32)


def dot_second(left, right):
    return lax.dot_general(left, right, (((1,), (1,)), ((), ())), preferred_element_type=f32)


class Bits:
    def __init__(self, batch, lat, items):
        group = lat // items
        self.batch, self.lat, self.items, self.group = batch, lat, items, group
        self.core = ("lat", 1, lat)
        self.zs = [("lat", 1 << k, lat) for k in range(1, group.bit_length() - 1)]
        self.item = [("lat", group << k, lat) for k in range(items.bit_length() - 1)]
        self.bs = [("batch", 1 << k, batch) for k in range(batch.bit_length() - 1)]


def swap(array, stage):
    name, mask, size = stage
    return lax.ppermute(array, name, [(i, i ^ mask) for i in range(size)])


def gather(array, stages):
    held = array[None]
    for stage in stages:
        held = jnp.concatenate([held, swap(held, stage)], axis=0)
    return held


def scatter(array, stages):
    for stage in reversed(stages):
        half = array.shape[0] // 2
        got = swap(array[half:], stage)
        array = (array[:half].astype(f32) + got.astype(f32)).astype(array.dtype)
    return array[0]


def spread(array, stages):
    held = array[:, None]
    for stage in reversed(stages):
        half = held.shape[0] // 2
        got = swap(held[half:], stage)
        held = jnp.stack([held[:half], got], axis=2)
        held = held.reshape((half, -1) + held.shape[3:])
    return held[0]


def slot_bits(position, stages, name):
    total = 0
    for place, (axis, mask, size) in enumerate(stages):
        if axis == name:
            total = total + jnp.where((position & mask) != 0, 1 << place, 0)
    return total


def slot_order(stages, bits):
    lat_far = jnp.arange(bits.lat, dtype=jnp.int32) ^ lax.axis_index("lat")
    batch_far = jnp.arange(bits.batch, dtype=jnp.int32) ^ lax.axis_index("batch")
    return (
        slot_bits(lat_far, stages, "lat")[:, None] + slot_bits(batch_far, stages, "batch")[None, :]
    )


def unpack(held, order, rows, columns):
    lat, batch = order.shape
    picked = jnp.take(held, order.reshape(-1), axis=0).reshape(lat, batch, rows, columns)
    return picked.transpose(0, 2, 1, 3).reshape(lat * rows, batch * columns)


def pack(whole, order, rows, columns):
    lat, batch = order.shape
    split = whole.reshape(lat, rows, batch, columns).transpose(0, 2, 1, 3)
    split = split.reshape(lat * batch, rows, columns)
    back = jnp.argsort(order.reshape(-1))
    return jnp.take(split, back, axis=0)


def heads_of(matrix):
    rows, width = matrix.shape
    return matrix.reshape(rows, HEADS, width // HEADS).transpose(1, 0, 2)


def rows_of(heads):
    count, rows, dim = heads.shape
    return heads.transpose(1, 0, 2).reshape(rows, count * dim)


def attend(query, keys, values, permit):
    scale = 1.0 / math.sqrt(query.shape[-1])
    score = jnp.einsum("hqd,hkd->hqk", query, keys, preferred_element_type=f32) * scale
    score = jnp.where(permit[None], score, masked_score)
    top = jnp.max(score, axis=-1, keepdims=True)
    expo = jnp.exp(score - top)
    total = jnp.sum(expo, axis=-1, keepdims=True)
    mix = jnp.einsum("hqk,hkd->hqd", expo.astype(bf16), values, preferred_element_type=f32) / total
    return mix, (top + jnp.log(total))


def attend_back(query, keys, values, permit, mix, lse, grad):
    scale = 1.0 / math.sqrt(query.shape[-1])
    score = jnp.einsum("hqd,hkd->hqk", query, keys, preferred_element_type=f32) * scale
    prob = jnp.where(permit[None], jnp.exp(score - lse), 0.0)
    delta = jnp.sum(grad.astype(f32) * mix, axis=-1, keepdims=True)
    d_prob = jnp.einsum("hqd,hkd->hqk", grad, values, preferred_element_type=f32)
    d_score = (prob * (d_prob - delta)).astype(bf16)
    d_v = jnp.einsum("hqk,hqd->hkd", prob.astype(bf16), grad, preferred_element_type=f32)
    d_k = jnp.einsum("hqk,hqd->hkd", d_score, query, preferred_element_type=f32) * scale
    d_q = jnp.einsum("hqk,hkd->hqd", d_score, keys, preferred_element_type=f32) * scale
    return d_q, d_k, d_v


def take_own(array, bits):
    return lax.dynamic_index_in_dim(array, lax.axis_index("lat") // bits.group, 0, keepdims=False)


def item_rows(array, bits):
    mine = lax.axis_index("lat") // bits.group
    parts = []
    for far in range(bits.items):
        part = lax.dynamic_index_in_dim(array, mine ^ far, 0, keepdims=False)
        if far:
            part = swap(part, ("lat", far * bits.group, bits.lat))
        parts.append(part)
    return jnp.concatenate(parts, axis=0)


def band_rows(array, bits):
    mine = lax.axis_index("lat") // bits.group
    rows = array.shape[0] // bits.items
    parts = []
    for far in range(bits.items):
        part = array[far * rows : (far + 1) * rows]
        if far:
            part = swap(part, ("lat", far * bits.group, bits.lat))
        parts.append(part)
    stacked = jnp.stack(parts)
    order = jnp.arange(bits.items, dtype=jnp.int32) ^ mine
    return jnp.take(stacked, order, axis=0)


def per_device(bits, patches, levels, lead_index, lead_table, ada, qkv, out, up, down, cotangent):
    layers = qkv.shape[0]
    width = patches.shape[2]
    lat_at, batch_at = lax.axis_index("lat"), lax.axis_index("batch")
    mine = lat_at // bits.group
    full = bits.zs + bits.item + bits.bs + [bits.core]
    order = slot_order(full, bits)

    shards = (qkv, out, up, down)
    whole = [
        [
            unpack(gather(shard[layer], full), order, shard.shape[1], shard.shape[2])
            for shard in shards
        ]
        for layer in range(layers)
    ]

    table_rows, lat_cols = lead_table.shape
    lead_row = jnp.broadcast_to(lead_index.astype(f32)[None], (table_rows, bits.items))
    lead_row = jnp.concatenate([lead_table.astype(f32), lead_row], axis=1)
    got = gather(lead_row, bits.bs)
    batch_far = jnp.arange(bits.batch, dtype=jnp.int32)
    row_ids = ((batch_at ^ batch_far)[:, None] * table_rows + jnp.arange(table_rows)[None]).reshape(-1)
    table = got[:, :, :lat_cols].reshape(-1, lat_cols)
    leads = got[:, 0, lat_cols:].reshape(-1)
    hot = (leads[:, None] == row_ids[None, :].astype(f32)).astype(f32)
    embed = jnp.dot(hot, table, precision=highest)
    cond = jax.nn.silu(embed).astype(bf16)
    part = jnp.stack([low_dot(cond, ada[layer]) for layer in range(layers)], axis=1)
    columns = part.shape[-1]
    part = part.reshape(bits.batch, bits.items, layers, columns)
    part = jnp.take(part, mine ^ jnp.arange(bits.items, dtype=jnp.int32), axis=1)
    part = part.transpose(1, 0, 2, 3)
    part = scatter(part, bits.item)
    for stage in bits.zs + [bits.core]:
        part = part + swap(part, stage)
    part = spread(part, bits.bs)
    part = jnp.take(part, batch_at ^ jnp.arange(bits.batch, dtype=jnp.int32), axis=0)
    modulation = part.transpose(1, 0, 2).reshape(layers, 6, width)

    rows = item_rows(patches, bits)
    flags = item_rows((levels >= needed_levels).astype(bf16), bits)
    upstream = item_rows(cotangent, bits).astype(f32)
    near = bits.zs + [bits.core]
    key_flags = gather(flags, near).reshape(-1)
    count = rows.shape[0]
    place = jnp.arange(key_flags.shape[0], dtype=jnp.int32)
    permit = (key_flags[None, :] > 0.5) | (place[None, :] == jnp.arange(count)[:, None])

    stream = rows.astype(f32)
    saved = []
    for layer in range(layers):
        w_qkv, w_out, w_up, w_down = whole[layer]
        shift1, scale1, gate1, shift2, scale2, gate2 = [modulation[layer, k] for k in range(6)]
        attn_in = (layer_norm(stream) * (1.0 + scale1) + shift1).astype(bf16)
        qkv_rows = low_dot(attn_in, w_qkv).astype(bf16)
        pairs = gather(qkv_rows[:, width:], near).reshape(-1, 2 * width)
        query = heads_of(qkv_rows[:, :width])
        keys, values = heads_of(pairs[:, :width]), heads_of(pairs[:, width:])
        mix, lse = attend(query, keys, values, permit)
        attn_low = rows_of(mix).astype(bf16)
        branch1 = low_dot(attn_low, w_out)
        middle = stream + gate1 * branch1
        mlp_in = (layer_norm(middle) * (1.0 + scale2) + shift2).astype(bf16)
        up_proj = low_dot(mlp_in, w_up)
        gelu_low = gelu_tanh(up_proj).astype(bf16)
        branch2 = low_dot(gelu_low, w_down)
        result = middle + gate2 * branch2
        saved.append((stream, attn_in, query, keys, values, mix, lse, attn_low, branch1, middle, mlp_in, up_proj, gelu_low, branch2))
        stream = result
    output = band_rows(stream.astype(bf16), bits)

    grads = [None] * layers
    mods = [None] * layers
    for layer in reversed(range(layers)):
        w_qkv, w_out, w_up, w_down = whole[layer]
        shift1, scale1, gate1, shift2, scale2, gate2 = [modulation[layer, k] for k in range(6)]
        (stream, attn_in, query, keys, values, mix, lse, attn_low, branch1, middle, mlp_in, up_proj, gelu_low, branch2) = saved[layer]
        d_gate2 = jnp.sum(upstream * branch2, axis=0)
        d_branch2 = (gate2 * upstream).astype(bf16)
        g_down = dot_first(gelu_low, d_branch2)
        d_gelu = dot_second(d_branch2, w_down)
        d_up = gelu_back(up_proj, d_gelu).astype(bf16)
        g_up = dot_first(mlp_in, d_up)
        d_mlp = dot_second(d_up, w_up)
        d_shift2 = jnp.sum(d_mlp, axis=0)
        d_scale2 = jnp.sum(d_mlp * layer_norm(middle), axis=0)
        d_mid = upstream + norm_back(middle, d_mlp * (1.0 + scale2))
        d_gate1 = jnp.sum(d_mid * branch1, axis=0)
        d_branch1 = (gate1 * d_mid).astype(bf16)
        g_out = dot_first(attn_low, d_branch1)
        d_attn = dot_second(d_branch1, w_out).astype(bf16)
        d_q, d_k, d_v = attend_back(query, keys, values, permit, mix, lse, heads_of(d_attn))
        pair = jnp.concatenate([rows_of(d_k), rows_of(d_v)], axis=1).astype(bf16)
        pair = scatter(pair.reshape(-1, count, 2 * width), near)
        d_qkv = jnp.concatenate([rows_of(d_q).astype(bf16), pair], axis=1)
        g_qkv = dot_first(attn_in, d_qkv)
        d_in = dot_second(d_qkv, w_qkv)
        d_shift1 = jnp.sum(d_in, axis=0)
        d_scale1 = jnp.sum(d_in * layer_norm(stream), axis=0)
        upstream = d_mid + norm_back(stream, d_in * (1.0 + scale1))
        mods[layer] = jnp.stack([d_shift1, d_scale1, d_gate1, d_shift2, d_scale2, d_gate2])
        grads[layer] = [
            scatter(pack(g.astype(bf16), order, s.shape[1], s.shape[2]), full).astype(f32)
            for g, s in zip((g_qkv, g_out, g_up, g_down), shards)
        ]
    patches_grad = band_rows(upstream.astype(bf16), bits)

    d_mod = jnp.stack(mods)
    for stage in near:
        d_mod = d_mod + swap(d_mod, stage)
    d_mod = gather(d_mod, bits.item)
    d_mod = d_mod.reshape(bits.items, layers, bits.batch, columns).transpose(2, 0, 1, 3)
    d_mod = jnp.take(d_mod, batch_at ^ jnp.arange(bits.batch, dtype=jnp.int32), axis=0)
    d_mod = spread(d_mod, bits.bs)
    d_mod = jnp.take(d_mod, mine ^ jnp.arange(bits.items, dtype=jnp.int32), axis=1)
    d_mod = d_mod.reshape(-1, layers, columns)
    ada_grad = jnp.stack(
        [lax.dot_general(cond.astype(f32), d_mod[:, layer], (((0,), (0,)), ((), ())), precision=highest) for layer in range(layers)]
    )
    d_cond = sum(
        lax.dot_general(d_mod[:, layer], ada[layer].astype(f32), (((1,), (1,)), ((), ())), precision=highest)
        for layer in range(layers)
    )
    d_embed = jax.vjp(jax.nn.silu, embed)[1](d_cond)[0]
    table_part = lax.dot_general(hot, d_embed, (((0,), (0,)), ((), ())), precision=highest)
    table_grad = scatter(table_part.reshape(bits.batch, table_rows, lat_cols), bits.bs)
    return (
        output,
        patches_grad,
        table_grad,
        ada_grad,
        jnp.stack([g[0] for g in grads]),
        jnp.stack([g[1] for g in grads]),
        jnp.stack([g[2] for g in grads]),
        jnp.stack([g[3] for g in grads]),
    )


def solution(mesh):
    batch, lat = mesh.shape["batch"], mesh.shape["lat"]

    def run(*arrays):
        bits = Bits(batch, lat, arrays[0].shape[0] // batch)
        rows = P("batch", "lat", None)
        weight = P(None, "lat", "batch")
        return jax.shard_map(
            lambda *pieces: per_device(bits, *pieces),
            mesh=mesh,
            in_specs=(rows, P("batch", "lat"), P("batch"), P("batch", "lat"), weight, weight, weight, weight, weight, rows),
            out_specs=(rows, rows, P("batch", "lat"), weight, weight, weight, weight, weight),
            check_vma=False,
        )(*arrays)

    return run
```

time: 1470 us -> 556 us (0.38)
  local copies, waits for them, and re-layouts: 604 us -> 181 us
  blocking collectives: 292 us -> 0 us
  waiting for transfers between devices: 331 us -> 136 us
  starting transfers between devices: 2.66 us -> 98.4 us
  matrix products: 135 us -> 62.8 us
  between operations: 19.9 us -> 4.14 us
    unnamed x567 -> x407, local copies, waits for them, and re-layouts: 512 us -> 31.9 us
    unnamed x44 -> x0, waiting for transfers between devices: 331 us -> none
    all_gather x20 -> x0, blocking collectives: 276 us -> none  [the longest x4 62.7 us: attend_forward(): lax.all_gather(value_heads, 'lat', axis=1, tiled=True)]
    ppermute x0 -> x109, waiting for transfers between devices: none -> 136 us  [swap(): return lax.ppermute(array, name, [(i, i ^ mask) for i in range(size)])]
    ppermute x0 -> x109, starting transfers between devices: none -> 98.4 us  [swap(): return lax.ppermute(array, name, [(i, i ^ mask) for i in range(size)])]
    reshape x0 -> x31, local copies, waits for them, and re-layouts: none -> 55.5 us  [the longest x6 23.8 us: unpack(): return picked.transpose(0, 2, 1, 3).reshape(lat * rows, batch * columns)]
    dot_general x50 -> x28, matrix products: 85.7 us -> 42.7 us  [the longest x10 9.16 us: low_dot(): return jnp.dot(left, right, preferred_element_type=f32)]
    gather x0 -> x22, local copies, waits for them, and re-layouts: none -> 35.8 us  [the longest x8 15.9 us: unpack(): jnp.take(held, order.reshape(-1), axis=0).reshape(lat, batch, rows, columns)]
  transfers between devices with their start and end apart: 26 -> 109, of which waited for: 9 -> 48; matrix products, arithmetic and copies ran while one was open for 47% -> 41% of each run, Pallas kernels for 0% -> 0%
where the time goes in v1:
time: 556 us; the launch traced here: 549 us
  local copies, waits for them, and re-layouts  181 us (33%)
  waiting for transfers between devices  136 us (24%)
  starting transfers between devices  98.4 us (18%)
  other arithmetic  66.6 us (12%)
  matrix products  62.8 us (11%)
    ppermute x109, waiting for transfers between devices, swap(): return lax.ppermute(array, name, [(i, i ^ mask) for i in range(size)])  136 us
    ppermute x109, starting transfers between devices, swap(): return lax.ppermute(array, name, [(i, i ^ mask) for i in range(size)])  98.4 us
    unnamed x407, local copies, waits for them, and re-layouts  31.9 us
    reshape x6, local copies, waits for them, and re-layouts, unpack(): return picked.transpose(0, 2, 1, 3).reshape(lat * rows, batch * columns)  23.8 us
    concatenate x20, local copies, waits for them, and re-layouts, gather(): held = jnp.concatenate([held, swap(held, stage)], axis=0)  22.9 us
    reshape x16, local copies, waits for them, and re-layouts, pack(): split = whole.reshape(lat, rows, batch, columns).transpose(0, 2, 1, 3)  20.9 us
    gather x8, local copies, waits for them, and re-layouts, unpack(): jnp.take(held, order.reshape(-1), axis=0).reshape(lat, batch, rows, columns)  15.9 us
    gather x8, local copies, waits for them, and re-layouts, pack(): return jnp.take(split, back, axis=0)  15.8 us
  transfers between devices with their start and end apart: 109, of which 48 were waited for; matrix products, arithmetic and copies ran while one was open for 41% of the time, Pallas kernels for 0%

profile of v1, /device:TPU:0, one launch (start us, length us, event | category | flops | bytes accessed | tf_op | source)
XLA Modules:
  0.0 549.3 jit_solution(8150075566747260333)
XLA Ops:
  2.2 3.1 collective-permute-start.23
  9.3 3.1 collective-permute-start.8
  36.3 3.6 collective-permute-done.3
  40.4 2.5 collective-permute-start.19
  43.0 4.5 collective-permute-done.19
  47.8 4.5 collective-permute-done.41
  85.6 3.5 collective-permute-done.29
  129.8 5.5 collective-permute-done.48
  148.1 2.4 collective-permute-done.53
  170.7 3.3 gather_fusion.6
  176.1 3.3 gather_fusion.10
  179.4 3.4 broadcast_select_fusion.2
  182.8 3.2 copy.75
  186.0 3.8 reshape.564
  199.7 2.4 fusion.61
  207.3 11.0 %collective-permute-done.38 = bf16[1,256,768]{2,1,0:T(8,128)(2,1)S(1)} collective-permute-done((bf16[1,256,768]{2,1,0:T(8,128)(2,1)S(1)}, bf16[1,256,768]{2,1,0:T(8,128)(2,1)S(1)}, u32[]{:S(2)}, u32[]{:S(2)}) %collective-permute-start.38) | collective-permute-done | bytes 393248 | tf_op jit(solution)/shard_map/ppermute | solution.py:59
  232.9 14.4 %reshape.576 = bf16[1536,384]{0,1:T(8,128)(2,1)} reshape(bf16[8,192,4,96]{1,0,3,2:T(8,128)(2,1)} %bitcast.291) | data formatting | bytes 2359296 | tf_op jit(solution)/shard_map/reshape | solution.py:106
  255.0 2.5 fusion.60
  267.1 4.4 fusion.32
  271.6 2.6 multiply_convert_fusion.1
  277.5 2.5 copy.85
  280.8 2.9 fusion.38
  291.8 2.9 copy.103
  311.0 2.5 gather_fusion.17
  319.1 3.0 fusion.57
  334.2 4.8 multiply_convert_fusion
  342.4 2.3 fusion.35
  344.7 3.5 reshape.596
  349.7 3.5 gather_fusion.20
  370.4 2.8 reshape.586
  385.7 4.4 collective-permute-done.80
  390.6 4.1 collective-permute-done.85
  396.2 2.9 collective-permute-done.81
  400.6 2.6 collective-permute-done.86
  405.5 2.5 collective-permute-done.82
  410.2 2.5 collective-permute-done.87
  436.0 6.7 %collective-permute-done.105 = bf16[8,192,96]{2,1,0:T(8,128)(2,1)S(1)} collective-permute-done((bf16[8,192,96]{2,1,0:T(8,128)(2,1)S(1)}, bf16[8,192,96]{2,1,0:T(8,128)(2,1)S(1)}, u32[]{:S(2)}, u32[]{:S(2)}) %collective-permute-start.105) | collective-permute-done | bytes 294944 | tf_op jit(solution)/shard_map/ppermute | solution.py:59
  444.4 4.6 collective-permute-done.90
  450.7 4.2 collective-permute-done.95
  463.0 7.1 %collective-permute-done.102 = bf16[2,192,96]{2,1,0:T(8,128)(2,1)S(1)} collective-permute-done((bf16[2,192,96]{2,1,0:T(8,128)(2,1)S(1)}, bf16[2,192,96]{2,1,0:T(8,128)(2,1)S(1)}, u32[]{:S(2)}, u32[]{:S(2)}) %collective-permute-start.102) | collective-permute-done | bytes 73760 | tf_op jit(solution)/shard_map/ppermute | solution.py:59
  495.1 3.6 collective-permute-done.64
  500.5 3.1 collective-permute-done.65
  513.0 2.8 collective-permute-done.67
  517.1 2.3 collective-permute-done.68
  526.3 3.7 collective-permute-done.70
  530.7 2.5 collective-permute-done.75
  541.3 3.0 collective-permute-done.77
  545.2 3.2 collective-permute-done.78
  (964 shorter events, 361.8 us)
Async XLA Ops:
  2.2 55.5 %collective-permute-start.23 = (bf16[1,48,384]{2,1,0:T(8,128)(2,1)S(1)}, bf16[1,48,384]{2,1,0:T(8,128)(2,1)S(1)}, u32[]{:S(2)}, u32[]{:S(2)}) collective-permute-start(bf16[1,48,384]{2,1,0:T(8,128)(2,1)S(1)} %get-tuple-element.126), channel_id=1, source_target_pairs={{0,2},{1,3},{2,0},{3,1},{4,6},{5,7},{6,4},{7,5},{8,10},{9,11},{10,... | collective-permute-start | bytes 110600 | tf_op jit(solution)/shard_map/ppermute | solution.py:59
  5.2 54.7 %collective-permute-start.45 = (bf16[1,48,384]{2,1,0:T(8,128)(2,1)S(1)}, bf16[1,48,384]{2,1,0:T(8,128)(2,1)S(1)}, u32[]{:S(2)}, u32[]{:S(2)}) collective-permute-start(bf16[1,48,384]{2,1,0:T(8,128)(2,1)S(1)} %get-tuple-element.125), channel_id=1, source_target_pairs={{0,2},{1,3},{2,0},{3,1},{4,6},{5,7},{6,4},{7,5},{8,10},{9,11},{10,... | collective-permute-start | bytes 110600 | tf_op jit(solution)/shard_map/ppermute | solution.py:59
  6.6 27.9 %collective-permute-start.18 = (bf16[1,48,96]{2,1,0:T(8,128)(2,1)S(1)}, bf16[1,48,96]{2,1,0:T(8,128)(2,1)S(1)}, u32[]{:S(2)}, u32[]{:S(2)}) collective-permute-start(bf16[1,48,96]{2,1,0:T(8,128)(2,1)S(1)} %get-tuple-element.168), channel_id=1, source_target_pairs={{0,2},{1,3},{2,0},{3,1},{4,6},{5,7},{6,4},{7,5},{8,10},{9,11},{10,... | collective-permute-start | bytes 27656 | tf_op jit(solution)/shard_map/ppermute | solution.py:59
  8.6 26.4 %collective-permute-start.40 = (bf16[1,48,96]{2,1,0:T(8,128)(2,1)S(1)}, bf16[1,48,96]{2,1,0:T(8,128)(2,1)S(1)}, u32[]{:S(2)}, u32[]{:S(2)}) collective-permute-start(bf16[1,48,96]{2,1,0:T(8,128)(2,1)S(1)} %get-tuple-element.167), channel_id=1, source_target_pairs={{0,2},{1,3},{2,0},{3,1},{4,6},{5,7},{6,4},{7,5},{8,10},{9,11},{10,... | collective-permute-start | bytes 27656 | tf_op jit(solution)/shard_map/ppermute | solution.py:59
  34.5 17.9 %collective-permute-start.33 = (bf16[1,48,288]{2,1,0:T(8,128)(2,1)S(1)}, bf16[1,48,288]{2,1,0:T(8,128)(2,1)S(1)}, u32[]{:S(2)}, u32[]{:S(2)}) collective-permute-start(bf16[1,48,288]{2,1,0:T(8,128)(2,1)S(1)} %get-tuple-element.133), channel_id=1, source_target_pairs={{0,2},{1,3},{2,0},{3,1},{4,6},{5,7},{6,4},{7,5},{8,10},{9,11},{10,... | collective-permute-start | bytes 82952 | tf_op jit(solution)/shard_map/ppermute | solution.py:59
  40.0 43.8 %collective-permute-start = (bf16[128,384]{1,0:T(8,128)(2,1)}, bf16[128,384]{1,0:T(8,128)(2,1)S(1)}, u32[]{:S(2)}, u32[]{:S(2)}) collective-permute-start(bf16[128,384]{1,0:T(8,128)(2,1)} %get-tuple-element.96), channel_id=1, source_target_pairs={{0,4},{1,5},{2,6},{3,7},{4,0},{5,1},{6,2},{7,3},{8,12},{9,13},{10,... | collective-permute-start | bytes 294920 | tf_op jit(solution)/shard_map/ppermute | solution.py:59
  61.0 18.2 %collective-permute-start.12 = (bf16[2,48,288]{2,1,0:T(8,128)(2,1)S(1)}, bf16[2,48,288]{2,1,0:T(8,128)(2,1)S(1)}, u32[]{:S(2)}, u32[]{:S(2)}) collective-permute-start(bf16[2,48,288]{2,1,0:T(8,128)(2,1)S(1)} %pad_maximum_fusion.33), channel_id=1, source_target_pairs={{0,4},{1,5},{2,6},{3,7},{4,0},{5,1},{6,2},{7,3},{8,12},{9,13},{10,... | collective-permute-start | bytes 165896 | tf_op jit(solution)/shard_map/ppermute | solution.py:59
  66.2 15.1 %collective-permute-start.34 = (bf16[2,48,288]{2,1,0:T(8,128)(2,1)}, bf16[2,48,288]{2,1,0:T(8,128)(2,1)S(1)}, u32[]{:S(2)}, u32[]{:S(2)}) collective-permute-start(bf16[2,48,288]{2,1,0:T(8,128)(2,1)} %pad_maximum_fusion.35), channel_id=1, source_target_pairs={{0,4},{1,5},{2,6},{3,7},{4,0},{5,1},{6,2},{7,3},{8,12},{9,13},{10,... | collective-permute-start | bytes 165896 | tf_op jit(solution)/shard_map/ppermute | solution.py:59
  67.3 23.4 %collective-permute-start.24 = (bf16[2,48,384]{2,1,0:T(8,128)(2,1)}, bf16[2,48,384]{2,1,0:T(8,128)(2,1)S(1)}, u32[]{:S(2)}, u32[]{:S(2)}) collective-permute-start(bf16[2,48,384]{2,1,0:T(8,128)(2,1)} %pad_maximum_fusion.34), channel_id=1, source_target_pairs={{0,4},{1,5},{2,6},{3,7},{4,0},{5,1},{6,2},{7,3},{8,12},{9,13},{10,... | collective-permute-start | bytes 221192 | tf_op jit(solution)/shard_map/ppermute | solution.py:59
  76.7 15.5 %collective-permute-start.46 = (bf16[2,48,384]{2,1,0:T(8,128)(2,1)}, bf16[2,48,384]{2,1,0:T(8,128)(2,1)S(1)}, u32[]{:S(2)}, u32[]{:S(2)}) collective-permute-start(bf16[2,48,384]{2,1,0:T(8,128)(2,1)} %pad_maximum_fusion.36), channel_id=1, source_target_pairs={{0,4},{1,5},{2,6},{3,7},{4,0},{5,1},{6,2},{7,3},{8,12},{9,13},{10,... | collective-permute-start | bytes 221192 | tf_op jit(solution)/shard_map/ppermute | solution.py:59
  83.7 13.5 %collective-permute-start.21 = (bf16[8,48,96]{2,1,0:T(8,128)(2,1)S(1)}, bf16[8,48,96]{2,1,0:T(8,128)(2,1)S(1)}, u32[]{:S(2)}, u32[]{:S(2)}) collective-permute-start(bf16[8,48,96]{2,1,0:T(8,128)(2,1)S(1)} %pad_maximum_fusion.29), channel_id=1, source_target_pairs={{0,16},{8,24},{16,0},{24,8},{1,17},{9,25},{17,1},{25,9},{2,18},{10... | collective-permute-start | bytes 221192 | tf_op jit(solution)/shard_map/ppermute | solution.py:59
  102.0 13.4 %collective-permute-start.22 = (bf16[16,48,96]{2,1,0:T(8,128)(2,1)S(1)}, bf16[16,48,96]{2,1,0:T(8,128)(2,1)S(1)}, u32[]{:S(2)}, u32[]{:S(2)}) collective-permute-start(bf16[16,48,96]{2,1,0:T(8,128)(2,1)S(1)} %get-tuple-element.117), channel_id=1, source_target_pairs={{0,1},{1,0},{2,3},{3,2},{4,5},{5,4},{6,7},{7,6},{8,9},{9,8},{10,11... | collective-permute-start | bytes 442376 | tf_op jit(solution)/shard_map/ppermute | solution.py:59
  104.2 14.8 %collective-permute-start.44 = (bf16[16,48,96]{2,1,0:T(8,128)(2,1)}, bf16[16,48,96]{2,1,0:T(8,128)(2,1)}, u32[]{:S(2)}, u32[]{:S(2)}) collective-permute-start(bf16[16,48,96]{2,1,0:T(8,128)(2,1)} %get-tuple-element.113), channel_id=1, source_target_pairs={{0,1},{1,0},{2,3},{3,2},{4,5},{5,4},{6,7},{7,6},{8,9},{9,8},{10,11... | collective-permute-start | bytes 442376 | tf_op jit(solution)/shard_map/ppermute | solution.py:59
  106.2 15.3 %collective-permute-start.14 = (bf16[8,48,288]{2,1,0:T(8,128)(2,1)}, bf16[8,48,288]{2,1,0:T(8,128)(2,1)S(1)}, u32[]{:S(2)}, u32[]{:S(2)}) collective-permute-start(bf16[8,48,288]{2,1,0:T(8,128)(2,1)} %pad_maximum_fusion.14), channel_id=1, source_target_pairs={{0,16},{8,24},{16,0},{24,8},{1,17},{9,25},{17,1},{25,9},{2,18},{10... | collective-permute-start | bytes 663560 | tf_op jit(solution)/shard_map/ppermute | solution.py:59
  108.5 14.1 %collective-permute-start.36 = (bf16[8,48,288]{2,1,0:T(8,128)(2,1)}, bf16[8,48,288]{2,1,0:T(8,128)(2,1)}, u32[]{:S(2)}, u32[]{:S(2)}) collective-permute-start(bf16[8,48,288]{2,1,0:T(8,128)(2,1)} %pad_maximum_fusion.16), channel_id=1, source_target_pairs={{0,16},{8,24},{16,0},{24,8},{1,17},{9,25},{17,1},{25,9},{2,18},{10... | collective-permute-start | bytes 663560 | tf_op jit(solution)/shard_map/ppermute | solution.py:59
  110.6 18.3 %collective-permute-start.26 = (bf16[8,48,384]{2,1,0:T(8,128)(2,1)}, bf16[8,48,384]{2,1,0:T(8,128)(2,1)S(1)}, u32[]{:S(2)}, u32[]{:S(2)}) collective-permute-start(bf16[8,48,384]{2,1,0:T(8,128)(2,1)} %pad_maximum_fusion.15), channel_id=1, source_target_pairs={{0,16},{8,24},{16,0},{24,8},{1,17},{9,25},{17,1},{25,9},{2,18},{10... | collective-permute-start | bytes 884744 | tf_op jit(solution)/shard_map/ppermute | solution.py:59
  115.4 19.9 %collective-permute-start.48 = (bf16[8,48,384]{2,1,0:T(8,128)(2,1)}, bf16[8,48,384]{2,1,0:T(8,128)(2,1)}, u32[]{:S(2)}, u32[]{:S(2)}) collective-permute-start(bf16[8,48,384]{2,1,0:T(8,128)(2,1)} %pad_maximum_fusion.17), channel_id=1, source_target_pairs={{0,16},{8,24},{16,0},{24,8},{1,17},{9,25},{17,1},{25,9},{2,18},{10... | collective-permute-start | bytes 884744 | tf_op jit(solution)/shard_map/ppermute | solution.py:59
  119.0 26.9 %collective-permute-start.31 = (bf16[8,192,96]{2,1,0:T(8,128)(2,1)}, bf16[8,192,96]{2,1,0:T(8,128)(2,1)}, u32[]{:S(2)}, u32[]{:S(2)}) collective-permute-start(bf16[8,192,96]{2,1,0:T(8,128)(2,1)} %pad_maximum_fusion.8), channel_id=1, source_target_pairs={{0,16},{8,24},{16,0},{24,8},{1,17},{9,25},{17,1},{25,9},{2,18},{10... | collective-permute-start | bytes 884744 | tf_op jit(solution)/shard_map/ppermute | solution.py:59
  122.2 15.0 %collective-permute-start.15 = (bf16[16,48,288]{2,1,0:T(8,128)(2,1)}, bf16[16,48,288]{2,1,0:T(8,128)(2,1)S(1)}, u32[]{:S(2)}, u32[]{:S(2)}) collective-permute-start(bf16[16,48,288]{2,1,0:T(8,128)(2,1)} %get-tuple-element.83), channel_id=1, source_target_pairs={{0,1},{1,0},{2,3},{3,2},{4,5},{5,4},{6,7},{7,6},{8,9},{9,8},{10,11... | collective-permute-start | bytes 1327112 | tf_op jit(solution)/shard_map/ppermute | solution.py:59
  124.5 14.1 %collective-permute-start.37 = (bf16[16,48,288]{2,1,0:T(8,128)(2,1)}, bf16[16,48,288]{2,1,0:T(8,128)(2,1)}, u32[]{:S(2)}, u32[]{:S(2)}) collective-permute-start(bf16[16,48,288]{2,1,0:T(8,128)(2,1)} %get-tuple-element.79), channel_id=1, source_target_pairs={{0,1},{1,0},{2,3},{3,2},{4,5},{5,4},{6,7},{7,6},{8,9},{9,8},{10,11... | collective-permute-start | bytes 1327112 | tf_op jit(solution)/shard_map/ppermute | solution.py:59
  128.9 21.7 %collective-permute-start.53 = (bf16[8,192,96]{2,1,0:T(8,128)(2,1)}, bf16[8,192,96]{2,1,0:T(8,128)(2,1)}, u32[]{:S(2)}, u32[]{:S(2)}) collective-permute-start(bf16[8,192,96]{2,1,0:T(8,128)(2,1)} %pad_maximum_fusion.9), channel_id=1, source_target_pairs={{0,16},{8,24},{16,0},{24,8},{1,17},{9,25},{17,1},{25,9},{2,18},{10... | collective-permute-start | bytes 884744 | tf_op jit(solution)/shard_map/ppermute | solution.py:59
  135.3 20.6 %collective-permute-start.27 = (bf16[16,48,384]{2,1,0:T(8,128)(2,1)}, bf16[16,48,384]{2,1,0:T(8,128)(2,1)}, u32[]{:S(2)}, u32[]{:S(2)}) collective-permute-start(bf16[16,48,384]{2,1,0:T(8,128)(2,1)} %get-tuple-element.81), channel_id=1, source_target_pairs={{0,1},{1,0},{2,3},{3,2},{4,5},{5,4},{6,7},{7,6},{8,9},{9,8},{10,11... | collective-permute-start | bytes 1769480 | tf_op jit(solution)/shard_map/ppermute | solution.py:59
  137.2 22.7 %collective-permute-start.49 = (bf16[16,48,384]{2,1,0:T(8,128)(2,1)}, bf16[16,48,384]{2,1,0:T(8,128)(2,1)}, u32[]{:S(2)}, u32[]{:S(2)}) collective-permute-start(bf16[16,48,384]{2,1,0:T(8,128)(2,1)} %get-tuple-element.77), channel_id=1, source_target_pairs={{0,1},{1,0},{2,3},{3,2},{4,5},{5,4},{6,7},{7,6},{8,9},{9,8},{10,11... | collective-permute-start | bytes 1769480 | tf_op jit(solution)/shard_map/ppermute | solution.py:59
  145.9 18.1 %collective-permute-start.16 = (bf16[1,256,768]{2,1,0:T(8,128)(2,1)S(1)}, bf16[1,256,768]{2,1,0:T(8,128)(2,1)S(1)}, u32[]{:S(2)}, u32[]{:S(2)}) collective-permute-start(bf16[1,256,768]{2,1,0:T(8,128)(2,1)S(1)} %slice_bitcast_fusion.1), channel_id=1, source_target_pairs={{0,2},{1,3},{2,0},{3,1},{4,6},{5,7},{6,4},{7,5},{8,10},{9,11},{10,... | collective-permute-start | bytes 1179656 | tf_op jit(solution)/shard_map/ppermute | solution.py:59
  148.1 20.5 %collective-permute-start.32 = (bf16[16,192,96]{2,1,0:T(8,128)(2,1)}, bf16[16,192,96]{2,1,0:T(8,128)(2,1)}, u32[]{:S(2)}, u32[]{:S(2)}) collective-permute-start(bf16[16,192,96]{2,1,0:T(8,128)(2,1)} %get-tuple-element.75), channel_id=1, source_target_pairs={{0,1},{1,0},{2,3},{3,2},{4,5},{5,4},{6,7},{7,6},{8,9},{9,8},{10,11... | collective-permute-start | bytes 1769480 | tf_op jit(solution)/shard_map/ppermute | solution.py:59
  152.6 21.4 %collective-permute-start.54 = (bf16[16,192,96]{2,1,0:T(8,128)(2,1)}, bf16[16,192,96]{2,1,0:T(8,128)(2,1)}, u32[]{:S(2)}, u32[]{:S(2)}) collective-permute-start(bf16[16,192,96]{2,1,0:T(8,128)(2,1)} %get-tuple-element.73), channel_id=1, source_target_pairs={{0,1},{1,0},{2,3},{3,2},{4,5},{5,4},{6,7},{7,6},{8,9},{9,8},{10,11... | collective-permute-start | bytes 1769480 | tf_op jit(solution)/shard_map/ppermute | solution.py:59
  165.0 24.8 %collective-permute-start.17 = (bf16[2,256,768]{2,1,0:T(8,128)(2,1)}, bf16[2,256,768]{2,1,0:T(8,128)(2,1)}, u32[]{:S(2)}, u32[]{:S(2)}) collective-permute-start(bf16[2,256,768]{2,1,0:T(8,128)(2,1)} %pad_maximum_fusion.4), channel_id=1, source_target_pairs={{0,1},{1,0},{2,3},{3,2},{4,5},{5,4},{6,7},{7,6},{8,9},{9,8},{10,11... | collective-permute-start | bytes 2359304 | tf_op jit(solution)/shard_map/ppermute | solution.py:59
  219.3 28.8 %collective-permute-start.39 = (bf16[2,256,768]{2,1,0:T(8,128)(2,1)}, bf16[2,256,768]{2,1,0:T(8,128)(2,1)}, u32[]{:S(2)}, u32[]{:S(2)}) collective-permute-start(bf16[2,256,768]{2,1,0:T(8,128)(2,1)} %pad_maximum_fusion.5), channel_id=1, source_target_pairs={{0,1},{1,0},{2,3},{3,2},{4,5},{5,4},{6,7},{7,6},{8,9},{9,8},{10,11... | collective-permute-start | bytes 2359304 | tf_op jit(solution)/shard_map/ppermute | solution.py:59
  220.1 40.2 %collective-permute-start.56 = (bf16[128,384]{1,0:T(8,128)(2,1)}, bf16[128,384]{1,0:T(8,128)(2,1)}, u32[]{:S(2)}, u32[]{:S(2)}) collective-permute-start(bf16[128,384]{1,0:T(8,128)(2,1)} %get-tuple-element.88), channel_id=1, source_target_pairs={{0,4},{1,5},{2,6},{3,7},{4,0},{5,1},{6,2},{7,3},{8,12},{9,13},{10,... | collective-permute-start | bytes 294920 | tf_op jit(solution)/shard_map/ppermute | solution.py:59
  280.0 14.7 %collective-permute-start.57 = (bf16[2,256,768]{2,1,0:T(8,128)(2,1)}, bf16[2,256,768]{2,1,0:T(8,128)(2,1)}, u32[]{:S(2)}, u32[]{:S(2)}) collective-permute-start(bf16[2,256,768]{2,1,0:T(8,128)(2,1)} %bitcast.330), channel_id=1, source_target_pairs={{0,1},{1,0},{2,3},{3,2},{4,5},{5,4},{6,7},{7,6},{8,9},{9,8},{10,11... | collective-permute-start | bytes 2359304 | tf_op jit(solution)/shard_map/ppermute | solution.py:59
  297.0 19.0 %collective-permute-start.58 = (bf16[1,256,768]{2,1,0:T(8,128)(2,1)}, bf16[1,256,768]{2,1,0:T(8,128)(2,1)}, u32[]{:S(2)}, u32[]{:S(2)}) collective-permute-start(bf16[1,256,768]{2,1,0:T(8,128)(2,1)} %slice.687), channel_id=1, source_target_pairs={{0,2},{1,3},{2,0},{3,1},{4,6},{5,7},{6,4},{7,5},{8,10},{9,11},{10,... | collective-permute-start | bytes 1179656 | tf_op jit(solution)/shard_map/ppermute | solution.py:59
  355.9 64.8 %collective-permute-start.99 = (bf16[16,192,96]{2,1,0:T(8,128)(2,1)}, bf16[16,192,96]{2,1,0:T(8,128)(2,1)}, u32[]{:S(2)}, u32[]{:S(2)}) collective-permute-start(bf16[16,192,96]{2,1,0:T(8,128)(2,1)} %slice.763), channel_id=1, source_target_pairs={{0,1},{1,0},{2,3},{3,2},{4,5},{5,4},{6,7},{7,6},{8,9},{9,8},{10,11... | collective-permute-start | bytes 1769480 | tf_op jit(solution)/shard_map/ppermute | solution.py:59
  357.2 65.6 %collective-permute-start.104 = (bf16[16,192,96]{2,1,0:T(8,128)(2,1)}, bf16[16,192,96]{2,1,0:T(8,128)(2,1)}, u32[]{:S(2)}, u32[]{:S(2)}) collective-permute-start(bf16[16,192,96]{2,1,0:T(8,128)(2,1)} %slice.773), channel_id=1, source_target_pairs={{0,1},{1,0},{2,3},{3,2},{4,5},{5,4},{6,7},{7,6},{8,9},{9,8},{10,11... | collective-permute-start | bytes 1769480 | tf_op jit(solution)/shard_map/ppermute | solution.py:59
  362.6 63.2 %collective-permute-start.89 = (bf16[16,48,384]{2,1,0:T(8,128)(2,1)}, bf16[16,48,384]{2,1,0:T(8,128)(2,1)}, u32[]{:S(2)}, u32[]{:S(2)}) collective-permute-start(bf16[16,48,384]{2,1,0:T(8,128)(2,1)} %slice.743), channel_id=1, source_target_pairs={{0,1},{1,0},{2,3},{3,2},{4,5},{5,4},{6,7},{7,6},{8,9},{9,8},{10,11... | collective-permute-start | bytes 1769480 | tf_op jit(solution)/shard_map/ppermute | solution.py:59
  365.9 17.4 %collective-permute-start.79 = (bf16[16,48,96]{2,1,0:T(8,128)(2,1)}, bf16[16,48,96]{2,1,0:T(8,128)(2,1)}, u32[]{:S(2)}, u32[]{:S(2)}) collective-permute-start(bf16[16,48,96]{2,1,0:T(8,128)(2,1)} %slice.723), channel_id=1, source_target_pairs={{0,1},{1,0},{2,3},{3,2},{4,5},{5,4},{6,7},{7,6},{8,9},{9,8},{10,11... | collective-permute-start | bytes 442376 | tf_op jit(solution)/shard_map/ppermute | solution.py:59
  366.8 14.8 %collective-permute-start.55 = (bf16[128,384]{1,0:T(8,128)(2,1)}, bf16[128,384]{1,0:T(8,128)(2,1)}, u32[]{:S(2)}, u32[]{:S(2)}) collective-permute-start(bf16[128,384]{1,0:T(8,128)(2,1)} %get-tuple-element.90), channel_id=1, source_target_pairs={{0,4},{1,5},{2,6},{3,7},{4,0},{5,1},{6,2},{7,3},{8,12},{9,13},{10,... | collective-permute-start | bytes 294920 | tf_op jit(solution)/shard_map/ppermute | solution.py:59
  381.6 46.0 %collective-permute-start.94 = (bf16[16,48,384]{2,1,0:T(8,128)(2,1)}, bf16[16,48,384]{2,1,0:T(8,128)(2,1)}, u32[]{:S(2)}, u32[]{:S(2)}) collective-permute-start(bf16[16,48,384]{2,1,0:T(8,128)(2,1)} %slice.753), channel_id=1, source_target_pairs={{0,1},{1,0},{2,3},{3,2},{4,5},{5,4},{6,7},{7,6},{8,9},{9,8},{10,11... | collective-permute-start | bytes 1769480 | tf_op jit(solution)/shard_map/ppermute | solution.py:59
  424.2 18.5 %collective-permute-start.105 = (bf16[8,192,96]{2,1,0:T(8,128)(2,1)S(1)}, bf16[8,192,96]{2,1,0:T(8,128)(2,1)S(1)}, u32[]{:S(2)}, u32[]{:S(2)}) collective-permute-start(bf16[8,192,96]{2,1,0:T(8,128)(2,1)S(1)} %slice.775), channel_id=1, source_target_pairs={{0,16},{8,24},{16,0},{24,8},{1,17},{9,25},{17,1},{25,9},{2,18},{10... | collective-permute-start | bytes 884744 | tf_op jit(solution)/shard_map/ppermute | solution.py:59
  427.1 22.0 %collective-permute-start.90 = (bf16[8,48,384]{2,1,0:T(8,128)(2,1)S(1)}, bf16[8,48,384]{2,1,0:T(8,128)(2,1)S(1)}, u32[]{:S(2)}, u32[]{:S(2)}) collective-permute-start(bf16[8,48,384]{2,1,0:T(8,128)(2,1)S(1)} %slice.745), channel_id=1, source_target_pairs={{0,16},{8,24},{16,0},{24,8},{1,17},{9,25},{17,1},{25,9},{2,18},{10... | collective-permute-start | bytes 884744 | tf_op jit(solution)/shard_map/ppermute | solution.py:59
  428.9 26.0 %collective-permute-start.95 = (bf16[8,48,384]{2,1,0:T(8,128)(2,1)S(1)}, bf16[8,48,384]{2,1,0:T(8,128)(2,1)S(1)}, u32[]{:S(2)}, u32[]{:S(2)}) collective-permute-start(bf16[8,48,384]{2,1,0:T(8,128)(2,1)S(1)} %slice.755), channel_id=1, source_target_pairs={{0,16},{8,24},{16,0},{24,8},{1,17},{9,25},{17,1},{25,9},{2,18},{10... | collective-permute-start | bytes 884744 | tf_op jit(solution)/shard_map/ppermute | solution.py:59
  430.7 49.3 %collective-permute-start.60 = (bf16[1,256,768]{2,1,0:T(8,128)(2,1)S(1)}, bf16[1,256,768]{2,1,0:T(8,128)(2,1)S(1)}, u32[]{:S(2)}, u32[]{:S(2)}) collective-permute-start(bf16[1,256,768]{2,1,0:T(8,128)(2,1)S(1)} %slice.691), channel_id=1, source_target_pairs={{0,2},{1,3},{2,0},{3,1},{4,6},{5,7},{6,4},{7,5},{8,10},{9,11},{10,... | collective-permute-start | bytes 1179656 | tf_op jit(solution)/shard_map/ppermute | solution.py:59
  434.4 22.1 %collective-permute-start.101 = (bf16[4,192,96]{2,1,0:T(8,128)(2,1)S(1)}, bf16[4,192,96]{2,1,0:T(8,128)(2,1)S(1)}, u32[]{:S(2)}, u32[]{:S(2)}) collective-permute-start(bf16[4,192,96]{2,1,0:T(8,128)(2,1)S(1)} %slice.767), channel_id=1, source_target_pairs={{0,8},{8,0},{16,24},{24,16},{1,9},{9,1},{17,25},{25,17},{2,10},{10... | collective-permute-start | bytes 442376 | tf_op jit(solution)/shard_map/ppermute | solution.py:59
  442.9 16.1 %collective-permute-start.106 = (bf16[4,192,96]{2,1,0:T(8,128)(2,1)S(1)}, bf16[4,192,96]{2,1,0:T(8,128)(2,1)S(1)}, u32[]{:S(2)}, u32[]{:S(2)}) collective-permute-start(bf16[4,192,96]{2,1,0:T(8,128)(2,1)S(1)} %slice.777), channel_id=1, source_target_pairs={{0,8},{8,0},{16,24},{24,16},{1,9},{9,1},{17,25},{25,17},{2,10},{10... | collective-permute-start | bytes 442376 | tf_op jit(solution)/shard_map/ppermute | solution.py:59
  456.6 13.5 %collective-permute-start.102 = (bf16[2,192,96]{2,1,0:T(8,128)(2,1)S(1)}, bf16[2,192,96]{2,1,0:T(8,128)(2,1)S(1)}, u32[]{:S(2)}, u32[]{:S(2)}) collective-permute-start(bf16[2,192,96]{2,1,0:T(8,128)(2,1)S(1)} %slice.769), channel_id=1, source_target_pairs={{0,4},{1,5},{2,6},{3,7},{4,0},{5,1},{6,2},{7,3},{8,12},{9,13},{10,... | collective-permute-start | bytes 221192 | tf_op jit(solution)/shard_map/ppermute | solution.py:59
  459.8 13.8 %collective-permute-start.92 = (bf16[2,48,384]{2,1,0:T(8,128)(2,1)S(1)}, bf16[2,48,384]{2,1,0:T(8,128)(2,1)S(1)}, u32[]{:S(2)}, u32[]{:S(2)}) collective-permute-start(bf16[2,48,384]{2,1,0:T(8,128)(2,1)S(1)} %slice.749), channel_id=1, source_target_pairs={{0,4},{1,5},{2,6},{3,7},{4,0},{5,1},{6,2},{7,3},{8,12},{9,13},{10,... | collective-permute-start | bytes 221192 | tf_op jit(solution)/shard_map/ppermute | solution.py:59
  491.6 30.0 %collective-permute-start.69 = (bf16[16,48,288]{2,1,0:T(8,128)(2,1)}, bf16[16,48,288]{2,1,0:T(8,128)(2,1)}, u32[]{:S(2)}, u32[]{:S(2)}) collective-permute-start(bf16[16,48,288]{2,1,0:T(8,128)(2,1)} %slice.703), channel_id=1, source_target_pairs={{0,1},{1,0},{2,3},{3,2},{4,5},{5,4},{6,7},{7,6},{8,9},{9,8},{10,11... | collective-permute-start | bytes 1327112 | tf_op jit(solution)/shard_map/ppermute | solution.py:59
  492.9 30.5 %collective-permute-start.74 = (bf16[16,48,288]{2,1,0:T(8,128)(2,1)}, bf16[16,48,288]{2,1,0:T(8,128)(2,1)}, u32[]{:S(2)}, u32[]{:S(2)}) collective-permute-start(bf16[16,48,288]{2,1,0:T(8,128)(2,1)} %slice.713), channel_id=1, source_target_pairs={{0,1},{1,0},{2,3},{3,2},{4,5},{5,4},{6,7},{7,6},{8,9},{9,8},{10,11... | collective-permute-start | bytes 1327112 | tf_op jit(solution)/shard_map/ppermute | solution.py:59
  504.2 15.8 %collective-permute-start.61 = (bf16[128,384]{1,0:T(8,128)(2,1)S(1)}, bf16[128,384]{1,0:T(8,128)(2,1)S(1)}, u32[]{:S(2)}, u32[]{:S(2)}) collective-permute-start(bf16[128,384]{1,0:T(8,128)(2,1)S(1)} %get-tuple-element.86), channel_id=1, source_target_pairs={{0,4},{1,5},{2,6},{3,7},{4,0},{5,1},{6,2},{7,3},{8,12},{9,13},{10,... | collective-permute-start | bytes 294920 | tf_op jit(solution)/shard_map/ppermute | solution.py:59
  (250 other events, 2660.9 us)
